TPU v7x, 32 devices: a whole 2x2x4 slice. The times are simulated.
32 devices in a mesh: groups: 2 (over y), tile: 4 (over z), sect: 4 (over x, core).
Axes of the slice: x: 2, y: 2, z: 4, core: 2. Of those that a mesh axis runs over, the one named last changes fastest.
Arguments:
- labels: int32 [16, 128, 512], P(('groups', 'sect'), None, 'tile'), parts along dimension 0, may hold values from 0 to 15
- classes: int32 [16, 128, 512], P(('groups', 'sect'), None, 'tile'), parts along dimension 0, may hold values from 0 to 7
- positions: int32 [8], P('groups'), parts along dimension 0, may hold values from 0 to 127
- phase_table: float32 [8], replicated, may hold values from -3.140625 to 3.140625
- brightness: float32 [16], replicated, may hold values from 0.2 to 2
- prop_taps: float32 [2, 2, 129], replicated, may hold values from -1 to 1, as said below
- detect_taps: float32 [2, 129], replicated, may hold values from 0 to 1, as said below
Outputs:
- image: float32 [16, 128, 512], P(('groups', 'sect'), None, 'tile'), parts along dimension 0
There are 2 independent parts, one for each index of `groups`. A program takes and returns all parts, laid end to end along the dimension named above; an argument that names none is the same for every part. Nothing has to cross between parts.
Inputs may be any that keep to these rules, and one draw needn't show every extreme that they name: `prop_taps`: the squares of the 2 x 129 entries of each axis's propagation taps sum to 1. `detect_taps`: each axis's detection taps are positive and sum to 1.
All inputs are finite; a program needn't handle non-finite values.
Results may differ from a plain program's by a relative error of at most 0.0001.
Values sent between devices are 32-bit elements; how exact they have to be, the bound alone decides.
A program may use at most 64 MiB of HBM per device.

v0:
```python
import jax
import jax.numpy as jnp
from jax import lax
from jax.sharding import PartitionSpec as P

SHEET_WIDTH = 6.0
AMPLITUDE = 2.0


def padded_2(x, sides, width):
    for axis, dim in sides:
        count, length = (lax.axis_size(axis), x.shape[dim])
        up = [(i, (i + 1) % count) for i in range(count - 1)]
        down = [(j, i) for i, j in up]
        last = lax.slice_in_dim(x, length - width, length, axis=dim)
        first = lax.slice_in_dim(x, 0, width, axis=dim)
        before = lax.ppermute(last, axis, up)
        after = lax.ppermute(first, axis, down)
        x = jnp.concatenate([before, x, after], axis=dim)
    return x


def toeplitz(tap_rows, size_in, size_out, shift, period):
    count = tap_rows.shape[-1]
    inner = lax.broadcasted_iota(jnp.int32, (size_in, size_out), 0)
    outer = lax.broadcasted_iota(jnp.int32, (size_in, size_out), 1)
    offset = inner - outer + shift
    if period > 0:
        tap_place = lax.broadcasted_iota(jnp.int32, (count, period), 0)
        target = lax.broadcasted_iota(jnp.int32, (count, period), 1)
        folding = (jnp.mod(tap_place, period) == target).astype(tap_rows.dtype)
        table = jnp.einsum("...t,tj->...j", tap_rows, folding, precision=lax.Precision.HIGHEST)
        index = jnp.mod(offset, period)
        return jnp.take(table, index, axis=-1)
    index = jnp.clip(offset, 0, count - 1)
    valid = (offset >= 0) & (offset < count)
    values = jnp.take(tap_rows, index, axis=-1)
    return jnp.where(valid, values, jnp.zeros_like(values))


def complex_block(parts):
    real_part, imag_part = (parts[0], parts[1])
    return jnp.stack([jnp.stack([real_part, imag_part]), jnp.stack([-imag_part, real_part])])


def lookup(indices, table):
    total = jnp.zeros(indices.shape, jnp.float32)
    for entry in range(table.shape[0]):
        total = total + jnp.where(indices == entry, table[entry], 0.0)
    return total


def sheet_plane(position, y_cells, z_cells):
    place = lax.broadcasted_iota(jnp.int32, (y_cells, z_cells), 0).astype(jnp.float32)
    offset = (place - position.astype(jnp.float32)) / SHEET_WIDTH
    real_part = AMPLITUDE * jnp.exp(-offset * offset)
    return jnp.stack([real_part, jnp.zeros_like(real_part)])


def apply_phase(field, cosine, sine):
    real_part = field[..., 0, :, :]
    imag_part = field[..., 1, :, :]
    return jnp.stack(
        [real_part * cosine - imag_part * sine, real_part * sine + imag_part * cosine], axis=-3
    )


def along_y(field, y_band):
    return jnp.einsum(
        "cdio,...ciz->...doz",
        y_band,
        field,
        precision=lax.Precision.HIGHEST,
        preferred_element_type=jnp.float32,
    )


def along_z(field, z_band):
    return jnp.einsum(
        "...cyi,cdio->...dyo",
        field,
        z_band,
        precision=lax.Precision.HIGHEST,
        preferred_element_type=jnp.float32,
    )


def pick_entry(values, index):
    return jnp.sum(jnp.where(lax.iota(jnp.int32, values.shape[0]) == index, values, 0))


def beam_maps(maps, left_x, right_x):
    return jnp.stack(
        [
            lax.dynamic_index_in_dim(maps, left_x, 0, keepdims=False),
            lax.dynamic_index_in_dim(maps, right_x, 0, keepdims=False),
        ]
    )


def deposit(collected, field, weights, left_x, right_x):
    energy = field[:, 0] * field[:, 0] + field[:, 1] * field[:, 1]
    left_row = (
        lax.dynamic_index_in_dim(collected, left_x, 0, keepdims=False) + weights[0] * energy[0]
    )
    collected = lax.dynamic_update_index_in_dim(collected, left_row, left_x, 0)
    right_row = (
        lax.dynamic_index_in_dim(collected, right_x, 0, keepdims=False) + weights[1] * energy[1]
    )
    return lax.dynamic_update_index_in_dim(collected, right_row, right_x, 0)


def phase_maps(cosine, sine):
    return (cosine, sine, cosine, sine, None)


def run_slices(field, collected, maps, weights, x_cells, y_band, z_band, half_taps):
    cosine, sine, cos_wide, sin_wide, wide_band = maps
    last_x = x_cells - 1

    def slice_step(index, inner):
        beam_pair, gathered = inner
        right_x = last_x - index
        beam_pair = apply_phase(
            beam_pair, beam_maps(cosine, index, right_x), beam_maps(sine, index, right_x)
        )
        beam_pair = along_y(beam_pair, y_band)
        padded = padded_2(beam_pair, (("tile", 3),), half_taps)
        beam_pair = along_z(padded, z_band)
        return (beam_pair, deposit(gathered, beam_pair, weights, index, right_x))

    return lax.fori_loop(0, x_cells, slice_step, (field, collected))


def on_device(labels, classes, positions, phase_table, brightness, prop_taps, detect_taps):
    x_cells, y_cells, z_cells = labels.shape
    half_taps = prop_taps.shape[-1] // 2
    sections = lax.axis_size("sect")
    section = lax.axis_index("sect")
    position_count = positions.shape[0]
    y_band = complex_block(toeplitz(prop_taps[0], y_cells, y_cells, half_taps, y_cells))
    z_band = complex_block(toeplitz(prop_taps[1], z_cells + 2 * half_taps, z_cells, 0, 0))

    def is_live(index):
        return ((index >= 0) & (index < position_count)).astype(jnp.float32)

    every_class = lax.all_gather(classes, "sect", axis=0, tiled=True)
    all_x = every_class.shape[0]
    maps = phase_maps(
        lookup(every_class, jnp.cos(phase_table)), lookup(every_class, jnp.sin(phase_table))
    )
    rounds = (position_count + sections - 1) // sections

    def round_step(number, totals):
        index = number * sections + section
        weight = is_live(index)
        weights = jnp.stack([weight, weight])
        start = sheet_plane(pick_entry(positions, index), y_cells, z_cells)
        field = jnp.stack([start, start])
        _, totals = run_slices(field, totals, maps, weights, all_x, y_band, z_band, half_taps)
        return totals

    totals = lax.fori_loop(0, rounds, round_step, jnp.zeros((all_x, y_cells, z_cells), jnp.float32))
    collected = lax.psum_scatter(totals, "sect", scatter_dimension=0, tiled=True)
    excitation = lookup(labels, brightness) * collected
    blur_y = toeplitz(detect_taps[0], y_cells, y_cells, half_taps, y_cells)
    blurred = jnp.einsum(
        "io,xiz->xoz",
        blur_y,
        excitation,
        precision=lax.Precision.HIGHEST,
        preferred_element_type=jnp.float32,
    )
    padded = padded_2(blurred, (("tile", 2),), half_taps)
    blur_z = toeplitz(detect_taps[1], z_cells + 2 * half_taps, z_cells, 0, 0)
    return jnp.einsum(
        "xyi,io->xyo",
        padded,
        blur_z,
        precision=lax.Precision.HIGHEST,
        preferred_element_type=jnp.float32,
    )


def solution(mesh):
    in_specs = (
        P(("groups", "sect"), None, "tile"),
        P(("groups", "sect"), None, "tile"),
        P("groups"),
        P(),
        P(),
        P(),
        P(),
    )
    out_specs = P(("groups", "sect"), None, "tile")
    return jax.shard_map(
        on_device, mesh=mesh, in_specs=in_specs, out_specs=out_specs, check_vma=False
    )
```

profile of v0, /device:TPU:0, one launch (start us, length us, event | category | flops | bytes accessed | tf_op | source)
XLA Modules:
  0.0 620.5 jit_solution(2362041293282826913)
XLA Ops:
  7.7 54.5 %gather_fusion = f32[16384,2]{1,0:T(8,128)} fusion(f32[2,128]{0,1:T(8,128)S(1)} %copy.67, s32[16384]{0:T(1024)S(1)} %fusion.89), kind=kCustom, calls=%fused_computation | custom fusion | bytes 327680 | tf_op jit(solution)/shard_map/jit(_take)/gather | solution.py:34
  62.2 5.2 copy.68
  68.5 108.5 %gather_fusion.1 = f32[32768,2]{1,0:T(8,128)} fusion(f32[2,129]{0,1:T(8,128)S(1)} %bitcast.168, s32[32768]{0:T(1024)S(1)} %fusion.27), kind=kCustom, calls=%fused_computation.1 | custom fusion | bytes 655360 | tf_op jit(solution)/shard_map/jit(_take)/gather | solution.py:37
  176.9 9.7 %copy.71 = f32[256,128,2]{1,0,2:T(8,128)S(1)} copy(f32[256,128,2]{2,1,0:T(8,128)} %bitcast.169) | data formatting | bytes 524288 | tf_op jit(solution)/shard_map/jit(_take)/gather | solution.py:37
  186.8 8.6 %all_gather.3 = s32[8,128,128]{2,1,0:T(8,128)S(1)} all-gather(s32[2,128,128]{2,1,0:T(8,128)S(1)} %copy-done.1), channel_id=1, replica_groups=mesh['groups'=2,'tile'=4,'sect'=4] {'sect'}, dimensions={0}, use_global_device_ids=true | all-gather | bytes 655360 | tf_op jit(solution)/shard_map/all_gather | solution.py:147
  196.1 5.8 select_add_fusion
  202.0 5.6 select_add_fusion.1
  209.7 84.3 %while.25 = (s32[]{:T(128)}, f32[2,2,128,128]{3,2,1,0:T(8,128)S(1)}, f32[8,128,128]{2,1,0:T(8,128)S(1)}, f32[8,128,128]{1,2,0:T(8,128)S(1)}, f32[8,128,128]{1,2,...) while((s32[]{:T(128)}, ...), condition=%wide.region_2.3_spmd, body=%wide.region_1.2_spmd.sunk | while | flops 604733440 | bytes 6291731 | solution.py:132
  210.3 1.3 collective-permute-start
  211.6 4.6 collective-permute-start.1
  216.2 1.8 collective-permute-done
  220.9 1.3 collective-permute-start
  222.2 5.0 collective-permute-start.1
  228.2 1.5 collective-permute-done.1
  232.7 5.0 collective-permute-start.1
  238.7 1.5 collective-permute-done.1
  242.0 1.3 collective-permute-start
  243.3 5.0 collective-permute-start.1
  249.3 1.5 collective-permute-done.1
  252.5 1.3 collective-permute-start
  253.8 5.0 collective-permute-start.1
  259.8 1.5 collective-permute-done.1
  264.3 5.0 collective-permute-start.1
  270.3 1.5 collective-permute-done.1
  274.8 5.0 collective-permute-start.1
  280.8 1.5 collective-permute-done.1
  285.4 5.0 collective-permute-start.1
  291.3 1.5 collective-permute-done.1
  295.0 97.2 %gather_fusion.2 = f32[16384]{0:T(1024)S(1)} fusion(f32[128]{0:T(128)S(1)} %convolution_bitcast_fusion.4, s32[16384]{0:T(1024)S(1)} %fusion.89), kind=kCustom, calls=%fused_computation.2 | custom fusion | bytes 196608 | tf_op jit(solution)/shard_map/jit(_take)/gather | solution.py:34
  393.0 11.4 %convolution_bitcast_fusion.2 = f32[2,128,128]{1,2,0:T(8,128)S(1)} fusion(f32[2,128,128]{2,1,0:T(8,128)} %reduce-scatter.2.cloned.1.call-done, s32[2,128,128]{2,1,0:T(8,128)S(1)} %copy-done.4, f32[16384]{0:T(1024)S(1)} %gather_fusion.2, f32[]{:T(128)} %bitcast.34, f32[]{:T(128)} %bitcast.33, f32[]{:T(128)} %bitcast.32, f32[]{:T(128)} %bitcast.31, ...), kind=kOutput, calls=%fused_computation.37 | convolution fusion | flops 52232192 | bytes 458816 | tf_op jit(solution)/shard_map/io,xiz->xoz/dot_general | solution.py:167
  404.5 4.4 collective-permute-start.2
  410.1 202.2 %gather_fusion.3 = f32[32768]{0:T(1024)S(1)} fusion(f32[129]{0:T(256)S(1)} %bitcast.167, s32[32768]{0:T(1024)S(1)} %fusion.27), kind=kCustom, calls=%fused_computation.3 | custom fusion | bytes 393216 | tf_op jit(solution)/shard_map/jit(_take)/gather | solution.py:37
  (139 shorter events, 35.1 us)
Async XLA Ops:
  6.5 180.2 %copy-start.5 = (f32[8]{0:T(128)S(1)}, f32[8]{0:T(128)}, u32[]{:S(2)}) copy-start(f32[8]{0:T(128)} %param.12) | copy-start | bytes 100
  6.5 180.2 %copy-start.1 = (s32[2,128,128]{2,1,0:T(8,128)S(1)}, s32[2,128,128]{2,1,0:T(8,128)}, u32[]{:S(2)}) copy-start(s32[2,128,128]{2,1,0:T(8,128)} %param.10) | copy-start | bytes 393220
  6.5 386.5 %reduce-scatter.2.cloned.1.call-start = ((), (), s32[]{:S(2)}) async-start(), calls=%async_computation.1 | async-start | bytes 655360 | tf_op jit(solution)/shard_map/reduce_scatter | solution.py:164
  62.2 145.8 %copy-start.6 = (s32[4]{0:T(128)S(1)}, s32[4]{0:T(128)}, u32[]{:S(2)}) copy-start(s32[4]{0:T(128)} %param.11) | copy-start | bytes 52
  207.6 87.2 %copy-start.3 = (f32[2,129]{1,0:T(2,128)S(1)}, f32[2,129]{1,0:T(2,128)}, u32[]{:S(2)}) copy-start(f32[2,129]{1,0:T(2,128)} %param.15) | copy-start | bytes 3100
  210.3 7.6 %collective-permute-start = (f32[2,2,128,64]{2,3,1,0:T(8,128)S(1)}, f32[2,2,128,64]{2,3,1,0:T(8,128)S(1)}, u32[]{:S(2)}, u32[]{:S(2)}) collective-permute-start(f32[2,2,128,64]{2,3,1,0:T(8,128)S(1)} %get-tuple-element.399), channel_id=1, source_target_pairs={{4,0},{8,4},{12,8},{5,1},{9,5},{13,9},{6,2},{10,6},{14,10},{7,3},{... | collective-permute-start | bytes 393224 | tf_op jit(solution)/shard_map/while/body/eval_jaxpr/while/body/eval_jaxpr/ppermute | solution.py:18
  211.6 7.5 %collective-permute-start.1 = (f32[2,2,128,64]{2,3,1,0:T(8,128)S(1)}, f32[2,2,128,64]{2,3,1,0:T(8,128)S(1)}, u32[]{:S(2)}, u32[]{:S(2)}) collective-permute-start(f32[2,2,128,64]{2,3,1,0:T(8,128)S(1)} %get-tuple-element.400), channel_id=1, source_target_pairs={{0,4},{4,8},{8,12},{1,5},{5,9},{9,13},{2,6},{6,10},{10,14},{3,7},{... | collective-permute-start | bytes 393224 | tf_op jit(solution)/shard_map/while/body/eval_jaxpr/while/body/eval_jaxpr/ppermute | solution.py:17
  220.9 7.3 %collective-permute-start = (f32[2,2,128,64]{2,3,1,0:T(8,128)S(1)}, f32[2,2,128,64]{2,3,1,0:T(8,128)S(1)}, u32[]{:S(2)}, u32[]{:S(2)}) collective-permute-start(f32[2,2,128,64]{2,3,1,0:T(8,128)S(1)} %get-tuple-element.399), channel_id=1, source_target_pairs={{4,0},{8,4},{12,8},{5,1},{9,5},{13,9},{6,2},{10,6},{14,10},{7,3},{... | collective-permute-start | bytes 393224 | tf_op jit(solution)/shard_map/while/body/eval_jaxpr/while/body/eval_jaxpr/ppermute | solution.py:18
  222.2 7.5 %collective-permute-start.1 = (f32[2,2,128,64]{2,3,1,0:T(8,128)S(1)}, f32[2,2,128,64]{2,3,1,0:T(8,128)S(1)}, u32[]{:S(2)}, u32[]{:S(2)}) collective-permute-start(f32[2,2,128,64]{2,3,1,0:T(8,128)S(1)} %get-tuple-element.400), channel_id=1, source_target_pairs={{0,4},{4,8},{8,12},{1,5},{5,9},{9,13},{2,6},{6,10},{10,14},{3,7},{... | collective-permute-start | bytes 393224 | tf_op jit(solution)/shard_map/while/body/eval_jaxpr/while/body/eval_jaxpr/ppermute | solution.py:17
  231.4 7.3 %collective-permute-start = (f32[2,2,128,64]{2,3,1,0:T(8,128)S(1)}, f32[2,2,128,64]{2,3,1,0:T(8,128)S(1)}, u32[]{:S(2)}, u32[]{:S(2)}) collective-permute-start(f32[2,2,128,64]{2,3,1,0:T(8,128)S(1)} %get-tuple-element.399), channel_id=1, source_target_pairs={{4,0},{8,4},{12,8},{5,1},{9,5},{13,9},{6,2},{10,6},{14,10},{7,3},{... | collective-permute-start | bytes 393224 | tf_op jit(solution)/shard_map/while/body/eval_jaxpr/while/body/eval_jaxpr/ppermute | solution.py:18
  232.7 7.5 %collective-permute-start.1 = (f32[2,2,128,64]{2,3,1,0:T(8,128)S(1)}, f32[2,2,128,64]{2,3,1,0:T(8,128)S(1)}, u32[]{:S(2)}, u32[]{:S(2)}) collective-permute-start(f32[2,2,128,64]{2,3,1,0:T(8,128)S(1)} %get-tuple-element.400), channel_id=1, source_target_pairs={{0,4},{4,8},{8,12},{1,5},{5,9},{9,13},{2,6},{6,10},{10,14},{3,7},{... | collective-permute-start | bytes 393224 | tf_op jit(solution)/shard_map/while/body/eval_jaxpr/while/body/eval_jaxpr/ppermute | solution.py:17
  242.0 7.3 %collective-permute-start = (f32[2,2,128,64]{2,3,1,0:T(8,128)S(1)}, f32[2,2,128,64]{2,3,1,0:T(8,128)S(1)}, u32[]{:S(2)}, u32[]{:S(2)}) collective-permute-start(f32[2,2,128,64]{2,3,1,0:T(8,128)S(1)} %get-tuple-element.399), channel_id=1, source_target_pairs={{4,0},{8,4},{12,8},{5,1},{9,5},{13,9},{6,2},{10,6},{14,10},{7,3},{... | collective-permute-start | bytes 393224 | tf_op jit(solution)/shard_map/while/body/eval_jaxpr/while/body/eval_jaxpr/ppermute | solution.py:18
  243.3 7.5 %collective-permute-start.1 = (f32[2,2,128,64]{2,3,1,0:T(8,128)S(1)}, f32[2,2,128,64]{2,3,1,0:T(8,128)S(1)}, u32[]{:S(2)}, u32[]{:S(2)}) collective-permute-start(f32[2,2,128,64]{2,3,1,0:T(8,128)S(1)} %get-tuple-element.400), channel_id=1, source_target_pairs={{0,4},{4,8},{8,12},{1,5},{5,9},{9,13},{2,6},{6,10},{10,14},{3,7},{... | collective-permute-start | bytes 393224 | tf_op jit(solution)/shard_map/while/body/eval_jaxpr/while/body/eval_jaxpr/ppermute | solution.py:17
  252.5 7.3 %collective-permute-start = (f32[2,2,128,64]{2,3,1,0:T(8,128)S(1)}, f32[2,2,128,64]{2,3,1,0:T(8,128)S(1)}, u32[]{:S(2)}, u32[]{:S(2)}) collective-permute-start(f32[2,2,128,64]{2,3,1,0:T(8,128)S(1)} %get-tuple-element.399), channel_id=1, source_target_pairs={{4,0},{8,4},{12,8},{5,1},{9,5},{13,9},{6,2},{10,6},{14,10},{7,3},{... | collective-permute-start | bytes 393224 | tf_op jit(solution)/shard_map/while/body/eval_jaxpr/while/body/eval_jaxpr/ppermute | solution.py:18
  253.8 7.5 %collective-permute-start.1 = (f32[2,2,128,64]{2,3,1,0:T(8,128)S(1)}, f32[2,2,128,64]{2,3,1,0:T(8,128)S(1)}, u32[]{:S(2)}, u32[]{:S(2)}) collective-permute-start(f32[2,2,128,64]{2,3,1,0:T(8,128)S(1)} %get-tuple-element.400), channel_id=1, source_target_pairs={{0,4},{4,8},{8,12},{1,5},{5,9},{9,13},{2,6},{6,10},{10,14},{3,7},{... | collective-permute-start | bytes 393224 | tf_op jit(solution)/shard_map/while/body/eval_jaxpr/while/body/eval_jaxpr/ppermute | solution.py:17
  263.0 7.3 %collective-permute-start = (f32[2,2,128,64]{2,3,1,0:T(8,128)S(1)}, f32[2,2,128,64]{2,3,1,0:T(8,128)S(1)}, u32[]{:S(2)}, u32[]{:S(2)}) collective-permute-start(f32[2,2,128,64]{2,3,1,0:T(8,128)S(1)} %get-tuple-element.399), channel_id=1, source_target_pairs={{4,0},{8,4},{12,8},{5,1},{9,5},{13,9},{6,2},{10,6},{14,10},{7,3},{... | collective-permute-start | bytes 393224 | tf_op jit(solution)/shard_map/while/body/eval_jaxpr/while/body/eval_jaxpr/ppermute | solution.py:18
  264.3 7.5 %collective-permute-start.1 = (f32[2,2,128,64]{2,3,1,0:T(8,128)S(1)}, f32[2,2,128,64]{2,3,1,0:T(8,128)S(1)}, u32[]{:S(2)}, u32[]{:S(2)}) collective-permute-start(f32[2,2,128,64]{2,3,1,0:T(8,128)S(1)} %get-tuple-element.400), channel_id=1, source_target_pairs={{0,4},{4,8},{8,12},{1,5},{5,9},{9,13},{2,6},{6,10},{10,14},{3,7},{... | collective-permute-start | bytes 393224 | tf_op jit(solution)/shard_map/while/body/eval_jaxpr/while/body/eval_jaxpr/ppermute | solution.py:17
  273.5 7.3 %collective-permute-start = (f32[2,2,128,64]{2,3,1,0:T(8,128)S(1)}, f32[2,2,128,64]{2,3,1,0:T(8,128)S(1)}, u32[]{:S(2)}, u32[]{:S(2)}) collective-permute-start(f32[2,2,128,64]{2,3,1,0:T(8,128)S(1)} %get-tuple-element.399), channel_id=1, source_target_pairs={{4,0},{8,4},{12,8},{5,1},{9,5},{13,9},{6,2},{10,6},{14,10},{7,3},{... | collective-permute-start | bytes 393224 | tf_op jit(solution)/shard_map/while/body/eval_jaxpr/while/body/eval_jaxpr/ppermute | solution.py:18
  274.8 7.5 %collective-permute-start.1 = (f32[2,2,128,64]{2,3,1,0:T(8,128)S(1)}, f32[2,2,128,64]{2,3,1,0:T(8,128)S(1)}, u32[]{:S(2)}, u32[]{:S(2)}) collective-permute-start(f32[2,2,128,64]{2,3,1,0:T(8,128)S(1)} %get-tuple-element.400), channel_id=1, source_target_pairs={{0,4},{4,8},{8,12},{1,5},{5,9},{9,13},{2,6},{6,10},{10,14},{3,7},{... | collective-permute-start | bytes 393224 | tf_op jit(solution)/shard_map/while/body/eval_jaxpr/while/body/eval_jaxpr/ppermute | solution.py:17
  284.1 7.3 %collective-permute-start = (f32[2,2,128,64]{2,3,1,0:T(8,128)S(1)}, f32[2,2,128,64]{2,3,1,0:T(8,128)S(1)}, u32[]{:S(2)}, u32[]{:S(2)}) collective-permute-start(f32[2,2,128,64]{2,3,1,0:T(8,128)S(1)} %get-tuple-element.399), channel_id=1, source_target_pairs={{4,0},{8,4},{12,8},{5,1},{9,5},{13,9},{6,2},{10,6},{14,10},{7,3},{... | collective-permute-start | bytes 393224 | tf_op jit(solution)/shard_map/while/body/eval_jaxpr/while/body/eval_jaxpr/ppermute | solution.py:18
  285.4 7.5 %collective-permute-start.1 = (f32[2,2,128,64]{2,3,1,0:T(8,128)S(1)}, f32[2,2,128,64]{2,3,1,0:T(8,128)S(1)}, u32[]{:S(2)}, u32[]{:S(2)}) collective-permute-start(f32[2,2,128,64]{2,3,1,0:T(8,128)S(1)} %get-tuple-element.400), channel_id=1, source_target_pairs={{0,4},{4,8},{8,12},{1,5},{5,9},{9,13},{2,6},{6,10},{10,14},{3,7},{... | collective-permute-start | bytes 393224 | tf_op jit(solution)/shard_map/while/body/eval_jaxpr/while/body/eval_jaxpr/ppermute | solution.py:17
  293.9 0.8 copy-start
  295.0 97.2 %copy-start.2 = (f32[16]{0:T(128)S(1)}, f32[16]{0:T(128)}, u32[]{:S(2)}) copy-start(f32[16]{0:T(128)} %param.13) | copy-start | bytes 196
  295.0 98.0 %copy-start.4 = (s32[2,128,128]{2,1,0:T(8,128)S(1)}, s32[2,128,128]{2,1,0:T(8,128)}, u32[]{:S(2)}) copy-start(s32[2,128,128]{2,1,0:T(8,128)} %param.9) | copy-start | bytes 393220
  404.5 207.9 %collective-permute-start.2 = (f32[2,128,64]{1,2,0:T(8,128)S(1)}, f32[2,128,64]{1,2,0:T(8,128)S(1)}, u32[]{:S(2)}, u32[]{:S(2)}) collective-permute-start(f32[2,128,64]{1,2,0:T(8,128)S(1)} %get-tuple-element.286), channel_id=1, source_target_pairs={{0,4},{4,8},{8,12},{1,5},{5,9},{9,13},{2,6},{6,10},{10,14},{3,7},{... | collective-permute-start | bytes 196616 | tf_op jit(solution)/shard_map/ppermute | solution.py:17
  408.8 203.6 %collective-permute-start.3 = (f32[2,128,64]{1,2,0:T(8,128)S(1)}, f32[2,128,64]{1,2,0:T(8,128)S(1)}, u32[]{:S(2)}, u32[]{:S(2)}) collective-permute-start(f32[2,128,64]{1,2,0:T(8,128)S(1)} %get-tuple-element.287), channel_id=1, source_target_pairs={{4,0},{8,4},{12,8},{5,1},{9,5},{13,9},{6,2},{10,6},{14,10},{7,3},{... | collective-permute-start | bytes 196616 | tf_op jit(solution)/shard_map/ppermute | solution.py:18
Sparse Core Ops, SparseCore 0:
  294.9 24.2 reduce-scatter.1
where the time goes:
time: 622 us; the launch traced here: 620 us
  local copies, waits for them, and re-layouts  482 us (77%)
  starting transfers between devices  55.5 us (9%)
  matrix products  24.9 us (4%)
  waiting for transfers between devices  20.5 us (3%)
  between operations  14.4 us (2%)
  other arithmetic  13.3 us (2%)
  blocking collectives  8.65 us (1%)
    gather x3, local copies, waits for them, and re-layouts, toeplitz(): values = jnp.take(tap_rows, index, axis=-1)  320 us
    gather x3, local copies, waits for them, and re-layouts, toeplitz(): return jnp.take(table, index, axis=-1)  157 us
    ppermute x9, starting transfers between devices, padded_2(): before = lax.ppermute(last, axis, up)  43.8 us
  transfers between devices with their start and end apart: 19, of which 16 were waited for; matrix products, arithmetic and copies ran while one was open for 48% of the time, Pallas kernels for 0%

commit v1 on v0

v1 whole, which is shorter than its diff:
```python
import functools
import jax
import jax.numpy as jnp
from jax import lax
from jax.experimental import pallas as pl
from jax.experimental.pallas import tpu as pltpu
from jax.sharding import PartitionSpec as P

SHEET_WIDTH = 6.0
AMPLITUDE = 2.0
F32 = jnp.float32
BF16 = jnp.bfloat16


def padded_2(x, sides, width):
    for axis, dim in sides:
        count, length = (lax.axis_size(axis), x.shape[dim])
        up = [(i, (i + 1) % count) for i in range(count - 1)]
        down = [(j, i) for i, j in up]
        last = lax.slice_in_dim(x, length - width, length, axis=dim)
        first = lax.slice_in_dim(x, 0, width, axis=dim)
        before = lax.ppermute(last, axis, up)
        after = lax.ppermute(first, axis, down)
        x = jnp.concatenate([before, x, after], axis=dim)
    return x


def lookup(indices, table):
    total = jnp.zeros(indices.shape, jnp.float32)
    for entry in range(table.shape[0]):
        total = total + jnp.where(indices == entry, table[entry], 0.0)
    return total


def split(x):
    high = x.astype(BF16)
    return high, (x - high.astype(F32)).astype(BF16)


def roll_rows(row, size, shift):
    return pltpu.roll(jnp.broadcast_to(row, (size, size)), shift, 1, stride=1, stride_axis=0)


def circulant(row, size, half):
    folded = row[:, :size] + row[:, size:]
    return roll_rows(folded, size, half % size)


def windows(row, size):
    rolled = roll_rows(row[:, :size], size, 0)
    outer = lax.broadcasted_iota(jnp.int32, (size, size), 0)
    inner = lax.broadcasted_iota(jnp.int32, (size, size), 1)
    last = jnp.broadcast_to(row[:, size:size + 1], (size, size))
    first = jnp.where(inner >= outer, rolled, 0.0)
    second = jnp.where(inner < outer, rolled, jnp.where(inner == outer, last, 0.0))
    return first.T, second.T


def select_tree(bits, values):
    while len(values) > 1:
        bit, bits = bits[0], bits[1:]
        values = [jnp.where(bit, values[i + 1], values[i]) for i in range(0, len(values), 2)]
    return values[0]


def bit_masks(indices, count):
    masks, step = [], 1
    while step < count:
        masks.append((indices & step) != 0)
        step *= 2
    return masks


def entries(row, count, shape):
    return [jnp.broadcast_to(row[:, k:k + 1], shape) for k in range(count)]


def kernel(tiles, cls_ref, pos_ref, phase_ref, prop_ref, detect_ref, out_ref, blur_y_ref, blur_z_ref,
           taps, trig, y_band, z_band, field, rolled, high, low):
    x_cells, size = out_ref.shape[0], out_ref.shape[1]
    own_x = cls_ref.shape[2]
    count = prop_ref.shape[-1]
    half = count // 2
    section, sections = lax.axis_index("sect"), lax.axis_size("sect")
    own_tile = lax.axis_index("tile")
    per_side = sections // 2
    beams = 2 * pos_ref.shape[0] // sections
    left = section < per_side

    taps[...] = jnp.zeros_like(taps)
    for axis in range(2):
        for part in range(2):
            n = 2 * axis + part
            taps[n:n + 1, 0:count] = prop_ref[axis, part:part + 1, :]
        taps[4 + axis:5 + axis, 0:count] = detect_ref[axis:axis + 1, :]

    y_re, y_im = (circulant(taps[n:n + 1, :], size, half) for n in (0, 1))
    y_all = jnp.concatenate([jnp.concatenate([y_re, -y_im], 1), jnp.concatenate([y_im, y_re], 1)], 0)
    y_high, y_low = split(y_all)
    y_band[...] = jnp.concatenate([y_high, y_low, y_high], 1)
    z_re, z_im = windows(taps[2:3, :], size), windows(taps[3:4, :], size)
    parts = []
    for side in range(2):
        top = jnp.concatenate([z_re[side], z_im[side]], 1)
        bottom = jnp.concatenate([-z_im[side], z_re[side]], 1)
        parts.append(split(jnp.concatenate([top, bottom], 0)))
    z_band[...] = jnp.concatenate([p[0] for p in parts] * 2 + [p[1] for p in parts], 0)
    blur_y_ref[...] = circulant(taps[4:5, :], size, half)
    b0, b1 = windows(taps[5:6, :], size)
    blur_z_ref[...] = jnp.concatenate([b0, b1], 0)

    classes = phase_ref.shape[1]
    trig[0:1, 0:classes] = jnp.cos(phase_ref[...])
    trig[1:2, 0:classes] = jnp.sin(phase_ref[...])
    place = lax.broadcasted_iota(jnp.int32, (size, size), 0).astype(F32)
    for b in range(beams):
        index = (section % per_side) * beams + b
        offset = (place - pos_ref[index].astype(F32)) / SHEET_WIDTH
        start = AMPLITUDE * jnp.exp(-offset * offset)

        @pl.loop(0, tiles)
        def _(j):
            field[j, b * size:(b + 1) * size, 0:size] = start
            field[j, b * size:(b + 1) * size, size:] = jnp.zeros_like(start)

    lane = lax.broadcasted_iota(jnp.int32, (size, size), 1)
    upper = lane < (size - half)
    unroll = tiles if tiles <= 4 else 1

    def shifted(j, before, now):
        joined = jnp.where(jnp.concatenate([jnp.concatenate([upper] * 2, 1)] * beams, 0), before, now)
        high[j], low[j] = split(joined)

    def slice_step(step, carry):
        x = jnp.where(left, step, x_cells - 1 - step)
        owner, inner = x // own_x, x % own_x
        cosines = entries(trig[0:1, :], classes, (size, size))
        sines = entries(trig[1:2, :], classes, (size, size))
        rolled[...] = jnp.zeros_like(rolled)

        def first(j, carry):
            masks = bit_masks(cls_ref[owner, j, inner], classes)
            cosine, sine = select_tree(masks, cosines), select_tree(masks, sines)
            reals, imags = [], []
            for b in range(beams):
                re = field[j, b * size:(b + 1) * size, 0:size]
                im = field[j, b * size:(b + 1) * size, size:]
                reals.append(re * cosine - im * sine)
                imags.append(re * sine + im * cosine)
            plane = jnp.concatenate([jnp.concatenate(reals, 1), jnp.concatenate(imags, 1)], 0)
            u_high, u_low = split(plane)
            v = jnp.dot(y_band[...], jnp.concatenate([u_high, u_high, u_low], 0), preferred_element_type=F32)
            rows = []
            for b in range(beams):
                cols = [pltpu.roll(v[c * size:(c + 1) * size, b * size:(b + 1) * size], half, 1) for c in range(2)]
                rows.append(jnp.concatenate(cols, 1))
            now = jnp.concatenate(rows, 0)
            shifted(j, rolled[...], now)
            rolled[...] = now
            return carry

        lax.fori_loop(0, tiles, first, 0, unroll=unroll)
        shifted(tiles, rolled[...], jnp.zeros_like(rolled))

        def second(j, carry):
            sides = [high[j], high[j + 1], low[j], low[j + 1], high[j], high[j + 1]]
            field[j] = jnp.dot(jnp.concatenate(sides, 1), z_band[...], preferred_element_type=F32)
            return carry

        lax.fori_loop(0, tiles, second, 0, unroll=unroll)
        w = field[own_tile]
        energy = w * w
        energy = energy[:, :size] + energy[:, size:]
        total = energy[0:size]
        for b in range(1, beams):
            total = total + energy[b * size:(b + 1) * size]
        out_ref[x] = total
        return carry

    lax.fori_loop(0, x_cells, slice_step, 0)


def on_device(labels, classes, positions, phase_table, brightness, prop_taps, detect_taps):
    own_x, size, _ = labels.shape
    half_taps = prop_taps.shape[-1] // 2
    sections, tiles = lax.axis_size("sect"), lax.axis_size("tile")
    x_cells = own_x * sections
    beams = 2 * positions.shape[0] // sections
    every_class = lax.all_gather(lax.all_gather(classes, "tile"), "sect")
    vmem, smem = pl.BlockSpec(memory_space=pltpu.VMEM), pl.BlockSpec(memory_space=pltpu.SMEM)
    rows = beams * size
    totals, blur_y, blur_z = pl.pallas_call(
        functools.partial(kernel, tiles),
        out_shape=(
            jax.ShapeDtypeStruct((x_cells, size, size), F32),
            jax.ShapeDtypeStruct((size, size), F32),
            jax.ShapeDtypeStruct((2 * size, size), F32),
        ),
        in_specs=[vmem, smem, vmem, vmem, vmem],
        out_specs=(vmem, vmem, vmem),
        scratch_shapes=[
            pltpu.VMEM((8, 2 * size), F32),
            pltpu.VMEM((8, 128), F32),
            pltpu.VMEM((2 * size, 6 * size), BF16),
            pltpu.VMEM((12 * size, 2 * size), BF16),
            pltpu.VMEM((tiles, rows, 2 * size), F32),
            pltpu.VMEM((rows, 2 * size), F32),
            pltpu.VMEM((tiles + 1, rows, 2 * size), BF16),
            pltpu.VMEM((tiles + 1, rows, 2 * size), BF16),
        ],
        compiler_params=pltpu.CompilerParams(vmem_limit_bytes=58 * 1024 * 1024),
    )(every_class, positions, phase_table.reshape(1, -1), prop_taps, detect_taps)
    collected = lax.psum_scatter(totals, "sect", scatter_dimension=0, tiled=True)
    excitation = lookup(labels, brightness) * collected
    blurred = jnp.einsum("yi,xiz->xyz", blur_y, excitation, precision=lax.Precision.HIGHEST,
                         preferred_element_type=F32)
    padded = padded_2(blurred, (("tile", 2),), half_taps)
    return jnp.einsum("xyi,io->xyo", padded, blur_z, precision=lax.Precision.HIGHEST,
                      preferred_element_type=F32)


def solution(mesh):
    in_specs = (
        P(("groups", "sect"), None, "tile"),
        P(("groups", "sect"), None, "tile"),
        P("groups"),
        P(),
        P(),
        P(),
        P(),
    )
    out_specs = P(("groups", "sect"), None, "tile")
    return jax.shard_map(
        on_device, mesh=mesh, in_specs=in_specs, out_specs=out_specs, check_vma=False
    )
```

time: 622 us -> 115 us (0.18)
  local copies, waits for them, and re-layouts: 482 us -> 0.74 us
  starting transfers between devices: 55.5 us -> 5.89 us
  waiting for transfers between devices: 20.5 us -> 45.7 us
  Pallas kernels: 0 us -> 17.1 us
  other arithmetic: 13.3 us -> 0 us
  matrix products: 24.9 us -> 12.8 us
  blocking collectives: 8.65 us -> 19.3 us
    gather x6 -> x0, local copies, waits for them, and re-layouts: 477 us -> none  [the longest x3 320 us: toeplitz(): values = jnp.take(tap_rows, index, axis=-1)]
    ppermute x9 -> x1, starting transfers between devices: 43.8 us -> 4.55 us  [padded_2(): before = lax.ppermute(last, axis, up)]
    all_gather x0 -> x1, waiting for transfers between devices: none -> 22.7 us  [on_device(): every_class = lax.all_gather(lax.all_gather(classes, 'tile'), 'sect')]
    reduce_scatter x1, waiting for transfers between devices: 0.02 us -> 21.1 us  [on_device(): lax.psum_scatter(totals, 'sect', scatter_dimension=0, tiled=True)]
    pallas_call x0 -> x1, Pallas kernels: none -> 17.1 us  [on_device(): pl.pallas_call(functools.partial(kernel, tiles), out_shape=(jax.ShapeDtyp...]
    dot_general x19 -> x1, matrix products: 23.6 us -> 11.6 us  [on_device(): jnp.einsum('yi,xiz->xyz', blur_y, excitation, precision=lax.Precision.HIG...]
    add x10 -> x0, other arithmetic: 11.6 us -> none  [the longest x2 11.4 us: lookup(): total = total + jnp.where(indices == entry, table[entry], 0.0)]
    all_gather x1, blocking collectives: 8.65 us -> 19.3 us  [on_device(): every_class = lax.all_gather(lax.all_gather(classes, 'tile'), 'sect')]
  transfers between devices with their start and end apart: 19 -> 4, of which waited for: 16 -> 4; matrix products, arithmetic and copies ran while one was open for 48% -> 1% of each run, Pallas kernels for 0% -> 0%
where the time goes in v1:
time: 115 us
  waiting for transfers between devices  45.7 us (40%)
  blocking collectives  19.3 us (17%)
  Pallas kernels  17.1 us (15%)
  between operations  13.4 us (12%)
  matrix products  12.8 us (11%)
  starting transfers between devices  5.89 us (5%)
    all_gather x1, waiting for transfers between devices, on_device(): every_class = lax.all_gather(lax.all_gather(classes, 'tile'), 'sect')  22.7 us
    reduce_scatter x1, waiting for transfers between devices, on_device(): lax.psum_scatter(totals, 'sect', scatter_dimension=0, tiled=True)  21.1 us
    all_gather x1, blocking collectives, on_device(): every_class = lax.all_gather(lax.all_gather(classes, 'tile'), 'sect')  19.3 us
    pallas_call x1, Pallas kernels, on_device(): pl.pallas_call(functools.partial(kernel, tiles), out_shape=(jax.ShapeDtyp...  17.1 us
    dot_general x1, matrix products, on_device(): jnp.einsum('yi,xiz->xyz', blur_y, excitation, precision=lax.Precision.HIG...  11.6 us
    ppermute x1, starting transfers between devices, padded_2(): before = lax.ppermute(last, axis, up)  4.55 us
  transfers between devices with their start and end apart: 4, of which 4 were waited for; matrix products, arithmetic and copies ran while one was open for 1% of the time, Pallas kernels for 0%

profile of v1, /device:TPU:0, one launch (start us, length us, event | category | flops | bytes accessed | tf_op | source)
XLA Modules:
  0.0 115.0 jit_solution(18364530240508799116)
XLA Ops:
  6.5 0.0 copy-start
  6.5 0.0 copy-start.2
  6.5 0.0 all-gather.4.cloned.1.call-start
  6.5 19.3 %all-gather = s32[8,128,128]{2,1,0:T(8,128)} all-gather(s32[2,128,128]{2,1,0:T(8,128)} %param.8), channel_id=2, replica_groups=mesh['groups'=2,'tile'=4,'sect'=4] {'tile'}, dimensions={0}, use_global_device_ids=true | all-gather | bytes 655360 | tf_op jit(solution)/shard_map/all_gather | solution.py:189
  25.9 0.0 all-gather.4.cloned.1.call-update
  25.9 0.0 reduce-scatter.2.cloned.1.call-start
  26.0 22.7 %all-gather.4.cloned.1.call-done = s32[16,2,128,128]{3,2,1,0:T(8,128)} async-done(((s32[4,2,128,128]{3,2,1,0:T(8,128)}), s32[16,2,128,128]{3,2,1,0:T(8,128)}) %all-gather.4.cloned.1.call-update) | async-done | bytes 2097168 | tf_op jit(solution)/shard_map/all_gather | solution.py:189
  48.7 17.1 %shard_map.73 = (f32[8,128,128]{2,1,0:T(8,128)}, f32[128,128]{1,0:T(8,128)}, f32[256,128]{1,0:T(8,128)}) custom-call(s32[4,4,2,128,128]{4,3,2,1,0:T(8,128)} %bitcast.28, s32[4]{0:T(128)} %pos_ref.1, f32[1,8]{1,0:T(1,128)} %bitcast.29, f32[2,2,129]{2,1,0:T(2,128)} %prop_ref.1, f32[2,129]{1,0:T(2,128)} %detect_ref.1), custom_call_target="tpu_custom_call" | custom-call | tf_op jit(solution)/shard_map/pallas_call | solution.py:192
  65.8 0.0 copy-start.1
  65.8 0.0 reduce-scatter.2.cloned.1.call-update
  65.8 0.0 copy-done
  65.8 0.7 fusion.108
  66.5 21.1 %reduce-scatter.2.cloned.1.call-done = f32[2,128,128]{2,1,0:T(8,128)} async-done(((f32[8,128,128]{2,1,0:T(8,128)}), f32[2,128,128]{2,1,0:T(8,128)}) %reduce-scatter.2.cloned.1.call-update) | async-done | bytes 131088 | tf_op jit(solution)/shard_map/reduce_scatter | solution.py:213
  87.6 0.0 copy-done.2
  87.6 11.6 %convolution_bitcast_fusion = f32[2,128,128]{1,2,0:T(8,128)S(1)} fusion(f32[2,128,128]{2,1,0:T(8,128)} %reduce-scatter.2.cloned.1.call-done, s32[2,128,128]{2,1,0:T(8,128)S(1)} %copy-done.2, f32[128,128]{1,0:T(8,128)} %get-tuple-element.9, f32[]{:T(128)} %bitcast.15, f32[]{:T(128)} %bitcast.14, f32[]{:T(128)} %bitcast.13, f32[]{:T(128)} %bitcast.12, ...), kind=kOutput, calls=%fused_computation | convolution fusion | flops 51904512 | bytes 458816 | tf_op jit(solution)/shard_map/yi,xiz->xyz/dot_general | solution.py:215
  99.2 1.3 %collective-permute-start.1 = (f32[2,128,64]{1,2,0:T(8,128)S(1)}, f32[2,128,64]{1,2,0:T(8,128)S(1)}, u32[]{:S(2)}, u32[]{:S(2)}) collective-permute-start(f32[2,128,64]{1,2,0:T(8,128)S(1)} %get-tuple-element.12), channel_id=1, source_target_pairs={{4,0},{8,4},{12,8},{5,1},{9,5},{13,9},{6,2},{10,6},{14,10},{7,3},{... | collective-permute-start | bytes 196616 | tf_op jit(solution)/shard_map/ppermute | solution.py:23
  100.5 4.5 %collective-permute-start = (f32[2,128,64]{1,2,0:T(8,128)S(1)}, f32[2,128,64]{1,2,0:T(8,128)S(1)}, u32[]{:S(2)}, u32[]{:S(2)}) collective-permute-start(f32[2,128,64]{1,2,0:T(8,128)S(1)} %get-tuple-element.11), channel_id=1, source_target_pairs={{0,4},{4,8},{8,12},{1,5},{5,9},{9,13},{2,6},{6,10},{10,14},{3,7},{... | collective-permute-start | bytes 196616 | tf_op jit(solution)/shard_map/ppermute | solution.py:22
  105.0 0.3 collective-permute-done.1
  105.3 1.6 %collective-permute-done = f32[2,128,64]{1,2,0:T(8,128)S(1)} collective-permute-done((f32[2,128,64]{1,2,0:T(8,128)S(1)}, f32[2,128,64]{1,2,0:T(8,128)S(1)}, u32[]{:S(2)}, u32[]{:S(2)}) %collective-permute-start) | collective-permute-done | bytes 65568 | tf_op jit(solution)/shard_map/ppermute | solution.py:22
  106.9 0.0 copy-done.1
  106.9 1.2 %fusion = f32[2,128,128]{2,1,0:T(8,128)} fusion(f32[2,128,64]{1,2,0:T(8,128)S(1)} %collective-permute-done.1, f32[2,128,128]{1,2,0:T(8,128)S(1)} %convolution_bitcast_fusion, f32[2,128,64]{1,2,0:T(8,128)S(1)} %collective-permute-done, f32[256,128]{1,0:T(8,128)S(1)} %copy-done.1), kind=kOutput, calls=%fused_computation.1 | convolution fusion | flops 100794368 | bytes 524288 | tf_op jit(solution)/shard_map/xyi,io->xyo/dot_general | solution.py:218
  (1 shorter events, 0.0 us)
Async XLA Ops:
  6.5 59.3 %copy-start = (f32[16]{0:T(128)S(1)}, f32[16]{0:T(128)}, u32[]{:S(2)}) copy-start(f32[16]{0:T(128)} %param.11) | copy-start | bytes 196
  6.5 81.1 %copy-start.2 = (s32[2,128,128]{2,1,0:T(8,128)S(1)}, s32[2,128,128]{2,1,0:T(8,128)}, u32[]{:S(2)}) copy-start(s32[2,128,128]{2,1,0:T(8,128)} %param.7) | copy-start | bytes 393220
  6.5 42.1 %all-gather.4.cloned.1.call-start = ((), (), s32[]{:S(2)}) async-start(), calls=%async_computation.2 | async-start | bytes 2621440 | tf_op jit(solution)/shard_map/all_gather | solution.py:189
  25.9 61.7 %reduce-scatter.2.cloned.1.call-start = ((), (), s32[]{:S(2)}) async-start(), calls=%async_computation.1 | async-start | bytes 655360 | tf_op jit(solution)/shard_map/reduce_scatter | solution.py:213
  65.8 41.2 %copy-start.1 = (f32[256,128]{1,0:T(8,128)S(1)}, f32[256,128]{1,0:T(8,128)}, u32[]{:S(2)}) copy-start(f32[256,128]{1,0:T(8,128)} %get-tuple-element.10) | copy-start | bytes 393220
  99.2 6.2 %collective-permute-start.1 = (f32[2,128,64]{1,2,0:T(8,128)S(1)}, f32[2,128,64]{1,2,0:T(8,128)S(1)}, u32[]{:S(2)}, u32[]{:S(2)}) collective-permute-start(f32[2,128,64]{1,2,0:T(8,128)S(1)} %get-tuple-element.12), channel_id=1, source_target_pairs={{4,0},{8,4},{12,8},{5,1},{9,5},{13,9},{6,2},{10,6},{14,10},{7,3},{... | collective-permute-start | bytes 196616 | tf_op jit(solution)/shard_map/ppermute | solution.py:23
  100.5 6.4 %collective-permute-start = (f32[2,128,64]{1,2,0:T(8,128)S(1)}, f32[2,128,64]{1,2,0:T(8,128)S(1)}, u32[]{:S(2)}, u32[]{:S(2)}) collective-permute-start(f32[2,128,64]{1,2,0:T(8,128)S(1)} %get-tuple-element.11), channel_id=1, source_target_pairs={{0,4},{4,8},{8,12},{1,5},{5,9},{9,13},{2,6},{6,10},{10,14},{3,7},{... | collective-permute-start | bytes 196616 | tf_op jit(solution)/shard_map/ppermute | solution.py:22
Sparse Core Ops, SparseCore 0:
  26.0 22.5 all-gather.3
  65.9 21.6 reduce-scatter.1

commit v2 on v1

--- a/solution.py
+++ b/solution.py
@@ -10,26 +10,7 @@
 AMPLITUDE = 2.0
 F32 = jnp.float32
 BF16 = jnp.bfloat16
-
-
-def padded_2(x, sides, width):
-    for axis, dim in sides:
-        count, length = (lax.axis_size(axis), x.shape[dim])
-        up = [(i, (i + 1) % count) for i in range(count - 1)]
-        down = [(j, i) for i, j in up]
-        last = lax.slice_in_dim(x, length - width, length, axis=dim)
-        first = lax.slice_in_dim(x, 0, width, axis=dim)
-        before = lax.ppermute(last, axis, up)
-        after = lax.ppermute(first, axis, down)
-        x = jnp.concatenate([before, x, after], axis=dim)
-    return x
-
-
-def lookup(indices, table):
-    total = jnp.zeros(indices.shape, jnp.float32)
-    for entry in range(table.shape[0]):
-        total = total + jnp.where(indices == entry, table[entry], 0.0)
-    return total
+MESH = pl.DeviceIdType.MESH
 
 
 def split(x):
@@ -75,17 +56,112 @@
     return [jnp.broadcast_to(row[:, k:k + 1], shape) for k in range(count)]
 
 
-def kernel(tiles, cls_ref, pos_ref, phase_ref, prop_ref, detect_ref, out_ref, blur_y_ref, blur_z_ref,
-           taps, trig, y_band, z_band, field, rolled, high, low):
-    x_cells, size = out_ref.shape[0], out_ref.shape[1]
-    own_x = cls_ref.shape[2]
+def dot3(a, b):
+    a_high, a_low = split(a)
+    b_high, b_low = split(b)
+    return jnp.dot(jnp.concatenate([a_high, a_low, a_high], 1), jnp.concatenate([b_high, b_high, b_low], 0),
+                   preferred_element_type=F32)
+
+
+def kernel(tiles, sections, labels_ref, classes_ref, pos_ref, phase_ref, bright_ref, prop_ref, detect_ref, out_ref,
+           held, label_held, taps, y_band, z_band, field, rolled, high, low, energy, gathered, edges, edge_in,
+           arrived, along, across, beside, label_sem, energy_out, energy_in, edge_out, edge_sem):
+    own_x, size = out_ref.shape[0], out_ref.shape[1]
+    x_cells = own_x * sections
     count = prop_ref.shape[-1]
     half = count // 2
-    section, sections = lax.axis_index("sect"), lax.axis_size("sect")
-    own_tile = lax.axis_index("tile")
+    section, tile = lax.axis_index("sect"), lax.axis_index("tile")
     per_side = sections // 2
     beams = 2 * pos_ref.shape[0] // sections
     left = section < per_side
+    place_in_side = section % per_side
+    mirror = (section + per_side) % sections
+    partners = [section - place_in_side + (place_in_side + m) % per_side for m in range(1, per_side)]
+
+    def tile_at(d):
+        return (tile + d) % tiles
+
+    def section_at(d):
+        return (section + d) % sections
+
+    barrier = pltpu.get_barrier_semaphore()
+
+    @pl.loop(1, tiles)
+    def _(d):
+        pl.semaphore_signal(barrier, inc=1, device_id={"tile": tile_at(d)}, device_id_type=MESH)
+
+    for d in range(1, sections):
+        pl.semaphore_signal(barrier, inc=1, device_id={"sect": section_at(d)}, device_id_type=MESH)
+    pl.semaphore_wait(barrier, tiles - 1 + sections - 1)
+
+    def own_copy(inner):
+        return pltpu.make_async_copy(
+            classes_ref.at[inner], held.at[section, inner, tile], arrived.at[section, inner, tile])
+
+    def slab_copy(source, owner, inner, j, sem, device):
+        return pltpu.make_async_remote_copy(
+            src_ref=source, dst_ref=held.at[owner, inner, j], send_sem=sem,
+            recv_sem=arrived.at[owner, inner, j], device_id=device, device_id_type=MESH)
+
+    def along_copy(inner, d):
+        return slab_copy(classes_ref.at[inner], section, inner, tile, along.at[inner, d], {"tile": tile_at(d)})
+
+    def mirror_copy(inner, j, source):
+        return slab_copy(source, section, inner, j, across.at[inner, j], {"sect": mirror})
+
+    def partner_copies(owner, kind, inner, j, source):
+        return [slab_copy(source, owner, inner, j, beside.at[kind, m, inner, j], {"sect": other})
+                for m, other in enumerate(partners)]
+
+    def await_slab(owner, inner, j):
+        slab_copy(held.at[owner, inner, j], owner, inner, j, across.at[inner, j], {"sect": mirror}).wait_recv()
+
+    def own_inner(n):
+        return jnp.where(left, n, own_x - 1 - n)
+
+    def mirror_inner(n):
+        return jnp.where(left, own_x - 1 - n, n)
+
+    for n in range(own_x):
+        inner = own_inner(n)
+        own_copy(inner).start()
+
+        @pl.loop(1, tiles)
+        def _(d):
+            along_copy(inner, d).start()
+
+        for copy in partner_copies(section, 0, inner, tile, classes_ref.at[inner]):
+            copy.start()
+        mirror_copy(inner, tile, classes_ref.at[inner]).start()
+    label_copy = pltpu.make_async_copy(labels_ref, label_held, label_sem)
+    label_copy.start()
+
+    def serve_own(n):
+        inner = own_inner(n)
+        own_copy(inner).wait()
+
+        @pl.loop(1, tiles)
+        def _(d):
+            j = tile_at(d)
+            await_slab(section, inner, j)
+            for copy in partner_copies(section, 0, inner, j, held.at[section, inner, j]):
+                copy.start()
+            mirror_copy(inner, j, held.at[section, inner, j]).start()
+
+    def serve_mirror(n):
+        inner = mirror_inner(n)
+
+        @pl.loop(0, tiles)
+        def _(j):
+            await_slab(mirror, inner, j)
+            for copy in partner_copies(mirror, 1, inner, j, held.at[mirror, inner, j]):
+                copy.start()
+
+    def energy_copy(x):
+        inner = x % own_x
+        return pltpu.make_async_remote_copy(
+            src_ref=energy.at[x], dst_ref=gathered.at[section, inner], send_sem=energy_out.at[x],
+            recv_sem=energy_in.at[section, inner], device_id={"sect": x // own_x}, device_id_type=MESH)
 
     taps[...] = jnp.zeros_like(taps)
     for axis in range(2):
@@ -105,16 +181,16 @@
         bottom = jnp.concatenate([-z_im[side], z_re[side]], 1)
         parts.append(split(jnp.concatenate([top, bottom], 0)))
     z_band[...] = jnp.concatenate([p[0] for p in parts] * 2 + [p[1] for p in parts], 0)
-    blur_y_ref[...] = circulant(taps[4:5, :], size, half)
-    b0, b1 = windows(taps[5:6, :], size)
-    blur_z_ref[...] = jnp.concatenate([b0, b1], 0)
-
-    classes = phase_ref.shape[1]
-    trig[0:1, 0:classes] = jnp.cos(phase_ref[...])
-    trig[1:2, 0:classes] = jnp.sin(phase_ref[...])
+
+    classes = phase_ref.shape[0]
+    spot = lax.broadcasted_iota(jnp.int32, (8, 128), 1)
+    phases = jnp.zeros((8, 128), F32)
+    for k in range(classes):
+        phases = jnp.where(spot == k, phase_ref[k], phases)
+    cos_row, sin_row = jnp.cos(phases)[0:1], jnp.sin(phases)[0:1]
     place = lax.broadcasted_iota(jnp.int32, (size, size), 0).astype(F32)
     for b in range(beams):
-        index = (section % per_side) * beams + b
+        index = place_in_side * beams + b
         offset = (place - pos_ref[index].astype(F32)) / SHEET_WIDTH
         start = AMPLITUDE * jnp.exp(-offset * offset)
 
@@ -131,15 +207,27 @@
         joined = jnp.where(jnp.concatenate([jnp.concatenate([upper] * 2, 1)] * beams, 0), before, now)
         high[j], low[j] = split(joined)
 
+    first_mirror = x_cells // 2 - own_x + 1
+
     def slice_step(step, carry):
         x = jnp.where(left, step, x_cells - 1 - step)
         owner, inner = x // own_x, x % own_x
-        cosines = entries(trig[0:1, :], classes, (size, size))
-        sines = entries(trig[1:2, :], classes, (size, size))
+        for n in range(own_x):
+            pl.when(step == n)(functools.partial(serve_own, n))
+            pl.when(step == first_mirror + n)(functools.partial(serve_mirror, n))
+
+        @pl.when(owner % per_side != place_in_side)
+        def _():
+            @pl.loop(0, tiles)
+            def _(j):
+                await_slab(owner, inner, j)
+
+        cosines = entries(cos_row, classes, (size, size))
+        sines = entries(sin_row, classes, (size, size))
         rolled[...] = jnp.zeros_like(rolled)
 
         def first(j, carry):
-            masks = bit_masks(cls_ref[owner, j, inner], classes)
+            masks = bit_masks(held[owner, inner, j], classes)
             cosine, sine = select_tree(masks, cosines), select_tree(masks, sines)
             reals, imags = [], []
             for b in range(beams):
@@ -168,55 +256,139 @@
             return carry
 
         lax.fori_loop(0, tiles, second, 0, unroll=unroll)
-        w = field[own_tile]
-        energy = w * w
-        energy = energy[:, :size] + energy[:, size:]
-        total = energy[0:size]
+        w = field[tile]
+        power = w * w
+        power = power[:, :size] + power[:, size:]
+        total = power[0:size]
         for b in range(1, beams):
-            total = total + energy[b * size:(b + 1) * size]
-        out_ref[x] = total
+            total = total + power[b * size:(b + 1) * size]
+        energy[x] = total
+        pl.when(owner != section)(lambda: energy_copy(x).start())
         return carry
 
     lax.fori_loop(0, x_cells, slice_step, 0)
+
+    blur_y = circulant(taps[4:5, :], size, half)
+    blur_z = jnp.concatenate(windows(taps[5:6, :], size), 0)
+    label_copy.wait()
+    lit = []
+    for inner in range(own_x):
+        masks = bit_masks(label_held[inner], bright_ref.shape[0])
+        lit.append(select_tree(masks, [jnp.full((size, size), bright_ref[k]) for k in range(bright_ref.shape[0])]))
+
+    def received(other, inner):
+        return pltpu.make_async_remote_copy(
+            src_ref=energy.at[0], dst_ref=gathered.at[other, inner], send_sem=energy_out.at[0],
+            recv_sem=energy_in.at[other, inner], device_id={"sect": other}, device_id_type=MESH)
+
+    columns = []
+    for inner in range(own_x):
+        total = energy[section * own_x + inner]
+        for d in range(1, sections):
+            received(section_at(d), inner).wait_recv()
+            total = total + gathered[section_at(d), inner]
+        columns.append(lit[inner] * total)
+    blurred = dot3(blur_y, jnp.concatenate(columns, 1))
+
+    top = lax.broadcasted_iota(jnp.int32, (size // 2, size), 1) < half
+    turned = []
+    for inner in range(own_x):
+        block = blurred[:, inner * size:(inner + 1) * size]
+        turn = pltpu.roll(block, half, 1)
+        turned.append(turn)
+        edges[0, inner] = jnp.where(top, turn[:size // 2], block[size // 2:])
+        edges[1, inner] = jnp.where(top, block[:size // 2], turn[size // 2:])
+
+    def edge_copy(way):
+        return pltpu.make_async_remote_copy(
+            src_ref=edges.at[way], dst_ref=edge_in.at[way], send_sem=edge_out.at[way],
+            recv_sem=edge_sem.at[way], device_id={"tile": tile_at(1 if way == 0 else tiles - 1)},
+            device_id_type=MESH)
+
+    has_next, has_before = tile < tiles - 1, tile > 0
+    edge_in_ok = (has_before, has_next)
+    edge_out_ok = (has_next, has_before)
+    for way in range(2):
+        pl.when(edge_out_ok[way])(lambda: edge_copy(way).start())
+    for way in range(2):
+        @pl.when(jnp.logical_not(edge_in_ok[way]))
+        def _():
+            edge_in[way] = jnp.zeros(edge_in.shape[1:], F32)
+
+        pl.when(edge_in_ok[way])(lambda: edge_copy(way).wait_recv())
+
+    planes = []
+    for inner in range(own_x):
+        turn = turned[inner]
+        before, after = edge_in[0, inner], edge_in[1, inner]
+        before = jnp.concatenate([before, pltpu.roll(before, half, 1)], 0)
+        after = jnp.concatenate([pltpu.roll(after, half, 1), after], 0)
+        planes.append(jnp.concatenate([jnp.where(upper, before, turn), jnp.where(upper, turn, after)], 1))
+    image = dot3(jnp.concatenate(planes, 0), blur_z)
+    for inner in range(own_x):
+        out_ref[inner] = image[inner * size:(inner + 1) * size]
+
+    for way in range(2):
+        pl.when(edge_out_ok[way])(lambda: edge_copy(way).wait_send())
+
+    @pl.loop(0, x_cells)
+    def _(x):
+        pl.when(x // own_x != section)(lambda: energy_copy(x).wait_send())
+
+    for inner in range(own_x):
+        @pl.loop(1, tiles)
+        def _(d):
+            along_copy(inner, d).wait_send()
+
+        @pl.loop(0, tiles)
+        def _(j):
+            mirror_copy(inner, j, held.at[section, inner, j]).wait_send()
+            for kind, owner in ((0, section), (1, mirror)):
+                for copy in partner_copies(owner, kind, inner, j, held.at[owner, inner, j]):
+                    copy.wait_send()
 
 
 def on_device(labels, classes, positions, phase_table, brightness, prop_taps, detect_taps):
     own_x, size, _ = labels.shape
-    half_taps = prop_taps.shape[-1] // 2
     sections, tiles = lax.axis_size("sect"), lax.axis_size("tile")
     x_cells = own_x * sections
     beams = 2 * positions.shape[0] // sections
-    every_class = lax.all_gather(lax.all_gather(classes, "tile"), "sect")
     vmem, smem = pl.BlockSpec(memory_space=pltpu.VMEM), pl.BlockSpec(memory_space=pltpu.SMEM)
+    anywhere = pl.BlockSpec(memory_space=pl.ANY)
     rows = beams * size
-    totals, blur_y, blur_z = pl.pallas_call(
-        functools.partial(kernel, tiles),
-        out_shape=(
-            jax.ShapeDtypeStruct((x_cells, size, size), F32),
-            jax.ShapeDtypeStruct((size, size), F32),
-            jax.ShapeDtypeStruct((2 * size, size), F32),
-        ),
-        in_specs=[vmem, smem, vmem, vmem, vmem],
-        out_specs=(vmem, vmem, vmem),
+    dma = pltpu.SemaphoreType.DMA
+    return pl.pallas_call(
+        functools.partial(kernel, tiles, sections),
+        out_shape=jax.ShapeDtypeStruct((own_x, size, size), F32),
+        in_specs=[anywhere, anywhere, smem, smem, smem, vmem, vmem],
+        out_specs=vmem,
         scratch_shapes=[
+            pltpu.VMEM((sections, own_x, tiles, size, size), jnp.int32),
+            pltpu.VMEM((own_x, size, size), jnp.int32),
             pltpu.VMEM((8, 2 * size), F32),
-            pltpu.VMEM((8, 128), F32),
             pltpu.VMEM((2 * size, 6 * size), BF16),
             pltpu.VMEM((12 * size, 2 * size), BF16),
             pltpu.VMEM((tiles, rows, 2 * size), F32),
             pltpu.VMEM((rows, 2 * size), F32),
             pltpu.VMEM((tiles + 1, rows, 2 * size), BF16),
             pltpu.VMEM((tiles + 1, rows, 2 * size), BF16),
+            pltpu.VMEM((x_cells, size, size), F32),
+            pltpu.VMEM((sections, own_x, size, size), F32),
+            pltpu.VMEM((2, own_x, size // 2, size), F32),
+            pltpu.VMEM((2, own_x, size // 2, size), F32),
+            dma((sections, own_x, tiles)),
+            dma((own_x, tiles)),
+            dma((own_x, tiles)),
+            dma((2, max(sections // 2 - 1, 1), own_x, tiles)),
+            dma,
+            dma((x_cells,)),
+            dma((sections, own_x)),
+            dma((2,)),
+            dma((2,)),
         ],
-        compiler_params=pltpu.CompilerParams(vmem_limit_bytes=58 * 1024 * 1024),
-    )(every_class, positions, phase_table.reshape(1, -1), prop_taps, detect_taps)
-    collected = lax.psum_scatter(totals, "sect", scatter_dimension=0, tiled=True)
-    excitation = lookup(labels, brightness) * collected
-    blurred = jnp.einsum("yi,xiz->xyz", blur_y, excitation, precision=lax.Precision.HIGHEST,
-                         preferred_element_type=F32)
-    padded = padded_2(blurred, (("tile", 2),), half_taps)
-    return jnp.einsum("xyi,io->xyo", padded, blur_z, precision=lax.Precision.HIGHEST,
-                      preferred_element_type=F32)
+        compiler_params=pltpu.CompilerParams(
+            vmem_limit_bytes=60 * 1024 * 1024, collective_id=0, has_side_effects=True),
+    )(labels, classes, positions, phase_table, brightness, prop_taps, detect_taps)
 
 
 def solution(mesh):

time: 115 us -> 43.7 us (0.38)
  waiting for transfers between devices: 45.7 us -> 0 us
  Pallas kernels: 17.1 us -> 42 us
  blocking collectives: 19.3 us -> 0 us
  between operations: 13.4 us -> 0.01 us
  matrix products: 12.8 us -> 0 us
  starting transfers between devices: 5.89 us -> 0 us
    pallas_call x1, Pallas kernels: 17.1 us -> 42 us  [on_device(): pl.pallas_call(functools.partial(kernel, tiles, sections), out_shape=jax....]
    all_gather x1 -> x0, waiting for transfers between devices: 22.7 us -> none  [on_device(): every_class = lax.all_gather(lax.all_gather(classes, 'tile'), 'sect')]
    reduce_scatter x1 -> x0, waiting for transfers between devices: 21.1 us -> none  [on_device(): lax.psum_scatter(totals, 'sect', scatter_dimension=0, tiled=True)]
    all_gather x1 -> x0, blocking collectives: 19.3 us -> none  [on_device(): every_class = lax.all_gather(lax.all_gather(classes, 'tile'), 'sect')]
    dot_general x2 -> x0, matrix products: 12.8 us -> none  [the longest x1 11.6 us: on_device(): jnp.einsum('yi,xiz->xyz', blur_y, excitation, precision=lax.Precision.HIG...]
    ppermute x2 -> x0, starting transfers between devices: 5.84 us -> none  [the longest x1 4.55 us: padded_2(): before = lax.ppermute(last, axis, up)]
    ppermute x2 -> x0, waiting for transfers between devices: 1.88 us -> none  [the longest x1 1.58 us: padded_2(): before = lax.ppermute(last, axis, up)]
    unnamed x6 -> x1, local copies, waits for them, and re-layouts: 0.01 us -> 1.57 us
  transfers between devices with their start and end apart: 4 -> 0, of which waited for: 4 -> 0; matrix products, arithmetic and copies ran while one was open for 1% -> 0% of each run, Pallas kernels for 0% -> 0%
where the time goes in v2:
time: 43.7 us; the launch traced here: 43.5 us
  Pallas kernels  42 us (96%)
  local copies, waits for them, and re-layouts  1.57 us (4%)
    pallas_call x1, Pallas kernels, on_device(): pl.pallas_call(functools.partial(kernel, tiles, sections), out_shape=jax....  42 us
    unnamed x1, local copies, waits for them, and re-layouts  1.57 us

profile of v2, /device:TPU:0, one launch (start us, length us, event | category | flops | bytes accessed | tf_op | source)
XLA Modules:
  0.0 43.5 jit_solution(3642050926590251231)
XLA Ops:
  0.0 42.0 %shard_map.73 = f32[2,128,128]{2,1,0:T(8,128)} custom-call(s32[2,128,128]{2,1,0:T(8,128)} %labels_ref.1, s32[2,128,128]{2,1,0:T(8,128)} %classes_ref.1, s32[4]{0:T(128)} %pos_ref.1, f32[8]{0:T(128)} %phase_ref.1, f32[16]{0:T(128)} %bright_ref.1, f32[2,2,129]{2,1,0:T(2,128)} %prop_ref.1, f32[2,129]{1,0:T(2,128)} %detect_ref.1), custom_call_target="tpu_custom_call" | custom-call | tf_op jit(solution)/shard_map/pallas_call | solution.py:360
  42.0 1.6 %copy.9 = f32[2,128,128]{2,1,0:T(8,128)} copy(f32[2,128,128]{2,1,0:T(8,128)} %shard_map.73) | data formatting | bytes 262144

commit v3 on v2

--- a/solution.py
+++ b/solution.py
@@ -65,7 +65,7 @@
 
 def kernel(tiles, sections, labels_ref, classes_ref, pos_ref, phase_ref, bright_ref, prop_ref, detect_ref, out_ref,
            held, label_held, taps, y_band, z_band, field, rolled, high, low, energy, gathered, edges, edge_in,
-           arrived, along, across, beside, label_sem, energy_out, energy_in, edge_out, edge_sem):
+           arrived, along, relay, across, beside, label_sem, energy_out, energy_in, edge_out, edge_sem):
     own_x, size = out_ref.shape[0], out_ref.shape[1]
     x_cells = own_x * sections
     count = prop_ref.shape[-1]
@@ -106,6 +106,10 @@
     def along_copy(inner, d):
         return slab_copy(classes_ref.at[inner], section, inner, tile, along.at[inner, d], {"tile": tile_at(d)})
 
+    def relay_copy(way, j, source):
+        other = tile_at(1 if way == 0 else tiles - 1)
+        return slab_copy(source, section, own_inner(0), j, relay.at[way, j], {"tile": other})
+
     def mirror_copy(inner, j, source):
         return slab_copy(source, section, inner, j, across.at[inner, j], {"sect": mirror})
 
@@ -116,37 +120,54 @@
     def await_slab(owner, inner, j):
         slab_copy(held.at[owner, inner, j], owner, inner, j, across.at[inner, j], {"sect": mirror}).wait_recv()
 
+    first_left, first_right = place_in_side == 0, place_in_side == per_side - 1
+    ascending = jnp.where(left, first_left, jnp.logical_not(first_right))
+    mirror_ascending = jnp.where(left, jnp.logical_not(first_right), first_left)
+    has_next, has_before = tile < tiles - 1, tile > 0
+
     def own_inner(n):
-        return jnp.where(left, n, own_x - 1 - n)
+        return jnp.where(ascending, n, own_x - 1 - n)
 
     def mirror_inner(n):
-        return jnp.where(left, own_x - 1 - n, n)
+        return jnp.where(mirror_ascending, n, own_x - 1 - n)
 
     for n in range(own_x):
         inner = own_inner(n)
         own_copy(inner).start()
-
-        @pl.loop(1, tiles)
-        def _(d):
-            along_copy(inner, d).start()
-
+        if n == 0:
+            pl.when(has_next)(lambda: relay_copy(0, tile, classes_ref.at[inner]).start())
+            pl.when(has_before)(lambda: relay_copy(1, tile, classes_ref.at[inner]).start())
         for copy in partner_copies(section, 0, inner, tile, classes_ref.at[inner]):
             copy.start()
         mirror_copy(inner, tile, classes_ref.at[inner]).start()
     label_copy = pltpu.make_async_copy(labels_ref, label_held, label_sem)
     label_copy.start()
 
+    def send_along():
+        for n in range(1, own_x):
+            @pl.loop(1, tiles)
+            def _(d):
+                along_copy(own_inner(n), d).start()
+
     def serve_own(n):
         inner = own_inner(n)
-        own_copy(inner).wait()
-
-        @pl.loop(1, tiles)
-        def _(d):
-            j = tile_at(d)
+
+        def arrival(j, way, onward):
             await_slab(section, inner, j)
+            if n == 0:
+                pl.when(onward)(lambda: relay_copy(way, j, held.at[section, inner, j]).start())
             for copy in partner_copies(section, 0, inner, j, held.at[section, inner, j]):
                 copy.start()
             mirror_copy(inner, j, held.at[section, inner, j]).start()
+
+        @pl.loop(1, tiles)
+        def _(d):
+            pl.when(tile - d >= 0)(lambda: arrival(tile - d, 0, has_next))
+            pl.when(tile + d < tiles)(lambda: arrival(tile + d, 1, has_before))
+            if n == 0:
+                pl.when(d == 1)(send_along)
+
+        own_copy(inner).wait()
 
     def serve_mirror(n):
         inner = mirror_inner(n)
@@ -207,14 +228,14 @@
         joined = jnp.where(jnp.concatenate([jnp.concatenate([upper] * 2, 1)] * beams, 0), before, now)
         high[j], low[j] = split(joined)
 
-    first_mirror = x_cells // 2 - own_x + 1
+    middle = x_cells // 2
 
     def slice_step(step, carry):
         x = jnp.where(left, step, x_cells - 1 - step)
         owner, inner = x // own_x, x % own_x
         for n in range(own_x):
             pl.when(step == n)(functools.partial(serve_own, n))
-            pl.when(step == first_mirror + n)(functools.partial(serve_mirror, n))
+            pl.when(step == (middle - 1 if n == 0 else middle + n if per_side > 1 else middle))(functools.partial(serve_mirror, n))
 
         @pl.when(owner % per_side != place_in_side)
         def _():
@@ -255,7 +276,14 @@
             field[j] = jnp.dot(jnp.concatenate(sides, 1), z_band[...], preferred_element_type=F32)
             return carry
 
-        lax.fori_loop(0, tiles, second, 0, unroll=unroll)
+        @pl.when(step < x_cells - 1)
+        def _():
+            lax.fori_loop(0, tiles, second, 0, unroll=unroll)
+
+        @pl.when(step == x_cells - 1)
+        def _():
+            second(tile, 0)
+
         w = field[tile]
         power = w * w
         power = power[:, :size] + power[:, size:]
@@ -305,7 +333,6 @@
             recv_sem=edge_sem.at[way], device_id={"tile": tile_at(1 if way == 0 else tiles - 1)},
             device_id_type=MESH)
 
-    has_next, has_before = tile < tiles - 1, tile > 0
     edge_in_ok = (has_before, has_next)
     edge_out_ok = (has_next, has_before)
     for way in range(2):
@@ -335,10 +362,18 @@
     def _(x):
         pl.when(x // own_x != section)(lambda: energy_copy(x).wait_send())
 
-    for inner in range(own_x):
-        @pl.loop(1, tiles)
-        def _(d):
-            along_copy(inner, d).wait_send()
+    @pl.loop(0, tiles)
+    def _(j):
+        source = held.at[section, own_inner(0), j]
+        pl.when(jnp.logical_and(has_next, j <= tile))(lambda: relay_copy(0, j, source).wait_send())
+        pl.when(jnp.logical_and(has_before, j >= tile))(lambda: relay_copy(1, j, source).wait_send())
+
+    for n in range(own_x):
+        inner = own_inner(n)
+        if n > 0:
+            @pl.loop(1, tiles)
+            def _(d):
+                along_copy(inner, d).wait_send()
 
         @pl.loop(0, tiles)
         def _(j):
@@ -378,6 +413,7 @@
             pltpu.VMEM((2, own_x, size // 2, size), F32),
             dma((sections, own_x, tiles)),
             dma((own_x, tiles)),
+            dma((2, tiles)),
             dma((own_x, tiles)),
             dma((2, max(sections // 2 - 1, 1), own_x, tiles)),
             dma,

time: 43.7 us -> 43.1 us (0.986)
  Pallas kernels: 42 us -> 41.2 us
    pallas_call x1, Pallas kernels: 42 us -> 41.2 us  [on_device(): pl.pallas_call(functools.partial(kernel, tiles, sections), out_shape=jax....]
where the time goes in v3:
time: 43.1 us; the launch traced here: 42.8 us
  Pallas kernels  41.2 us (96%)
  local copies, waits for them, and re-layouts  1.57 us (4%)
    pallas_call x1, Pallas kernels, on_device(): pl.pallas_call(functools.partial(kernel, tiles, sections), out_shape=jax....  41.2 us
    unnamed x1, local copies, waits for them, and re-layouts  1.57 us

profile of v3, /device:TPU:0, one launch (start us, length us, event | category | flops | bytes accessed | tf_op | source)
XLA Modules:
  0.0 42.8 jit_solution(11283595502938769135)
XLA Ops:
  0.0 41.2 %shard_map.73 = f32[2,128,128]{2,1,0:T(8,128)} custom-call(s32[2,128,128]{2,1,0:T(8,128)} %labels_ref.1, s32[2,128,128]{2,1,0:T(8,128)} %classes_ref.1, s32[4]{0:T(128)} %pos_ref.1, f32[8]{0:T(128)} %phase_ref.1, f32[16]{0:T(128)} %bright_ref.1, f32[2,2,129]{2,1,0:T(2,128)} %prop_ref.1, f32[2,129]{1,0:T(2,128)} %detect_ref.1), custom_call_target="tpu_custom_call" | custom-call | tf_op jit(solution)/shard_map/pallas_call | solution.py:395
  41.2 1.6 %copy.9 = f32[2,128,128]{2,1,0:T(8,128)} copy(f32[2,128,128]{2,1,0:T(8,128)} %shard_map.73) | data formatting | bytes 262144

commit v4 on v3

--- a/solution.py
+++ b/solution.py
@@ -65,7 +65,7 @@
 
 def kernel(tiles, sections, labels_ref, classes_ref, pos_ref, phase_ref, bright_ref, prop_ref, detect_ref, out_ref,
            held, label_held, taps, y_band, z_band, field, rolled, high, low, energy, gathered, edges, edge_in,
-           arrived, along, relay, across, beside, label_sem, energy_out, energy_in, edge_out, edge_sem):
+           arrived, along, spread, relay, across, beside, label_sem, energy_out, energy_in, edge_out, edge_sem):
     own_x, size = out_ref.shape[0], out_ref.shape[1]
     x_cells = own_x * sections
     count = prop_ref.shape[-1]
@@ -94,6 +94,11 @@
         pl.semaphore_signal(barrier, inc=1, device_id={"sect": section_at(d)}, device_id_type=MESH)
     pl.semaphore_wait(barrier, tiles - 1 + sections - 1)
 
+    def within(owner, inner, j, forward):
+        x = owner * own_x + inner
+        after = jnp.where(forward, x_cells - x, x + 1)
+        return jnp.abs(j - tile) <= (half * after + size - 1) // size
+
     def own_copy(inner):
         return pltpu.make_async_copy(
             classes_ref.at[inner], held.at[section, inner, tile], arrived.at[section, inner, tile])
@@ -109,6 +114,9 @@
     def relay_copy(way, j, source):
         other = tile_at(1 if way == 0 else tiles - 1)
         return slab_copy(source, section, own_inner(0), j, relay.at[way, j], {"tile": other})
+
+    def spread_copy(inner, d):
+        return slab_copy(held.at[mirror, inner, tile], mirror, inner, tile, spread.at[inner, d], {"tile": tile_at(d)})
 
     def mirror_copy(inner, j, source):
         return slab_copy(source, section, inner, j, across.at[inner, j], {"sect": mirror})
@@ -149,6 +157,17 @@
             def _(d):
                 along_copy(own_inner(n), d).start()
 
+        for n in range(1, own_x):
+            inner = mirror_inner(n)
+            await_slab(mirror, inner, tile)
+
+            @pl.loop(1, tiles)
+            def _(d):
+                pl.when(within(mirror, inner, tile_at(d), left))(lambda: spread_copy(inner, d).start())
+
+            for copy in partner_copies(mirror, 1, inner, tile, held.at[mirror, inner, tile]):
+                copy.start()
+
     def serve_own(n):
         inner = own_inner(n)
 
@@ -158,7 +177,10 @@
                 pl.when(onward)(lambda: relay_copy(way, j, held.at[section, inner, j]).start())
             for copy in partner_copies(section, 0, inner, j, held.at[section, inner, j]):
                 copy.start()
-            mirror_copy(inner, j, held.at[section, inner, j]).start()
+            if n == 0:
+                @pl.when(within(section, inner, j, jnp.logical_not(left)))
+                def _():
+                    mirror_copy(inner, j, held.at[section, inner, j]).start()
 
         @pl.loop(1, tiles)
         def _(d):
@@ -174,9 +196,13 @@
 
         @pl.loop(0, tiles)
         def _(j):
-            await_slab(mirror, inner, j)
-            for copy in partner_copies(mirror, 1, inner, j, held.at[mirror, inner, j]):
-                copy.start()
+            wanted = within(mirror, inner, j, left)
+
+            @pl.when(wanted if n == 0 else jnp.logical_and(wanted, j != tile))
+            def _():
+                await_slab(mirror, inner, j)
+                for copy in partner_copies(mirror, 1, inner, j, held.at[mirror, inner, j]):
+                    copy.start()
 
     def energy_copy(x):
         inner = x % own_x
@@ -241,7 +267,8 @@
         def _():
             @pl.loop(0, tiles)
             def _(j):
-                await_slab(owner, inner, j)
+                wanted = jnp.logical_or(step < middle, within(owner, inner, j, left))
+                pl.when(wanted)(lambda: await_slab(owner, inner, j))
 
         cosines = entries(cos_row, classes, (size, size))
         sines = entries(sin_row, classes, (size, size))
@@ -375,11 +402,27 @@
             def _(d):
                 along_copy(inner, d).wait_send()
 
+            mirror_copy(inner, tile, classes_ref.at[inner]).wait_send()
+            far = mirror_inner(n)
+
+            @pl.loop(1, tiles)
+            def _(d):
+                pl.when(within(mirror, far, tile_at(d), left))(lambda: spread_copy(far, d).wait_send())
+
         @pl.loop(0, tiles)
         def _(j):
-            mirror_copy(inner, j, held.at[section, inner, j]).wait_send()
-            for kind, owner in ((0, section), (1, mirror)):
-                for copy in partner_copies(owner, kind, inner, j, held.at[owner, inner, j]):
+            if n == 0:
+                @pl.when(within(section, inner, j, jnp.logical_not(left)))
+                def _():
+                    mirror_copy(inner, j, held.at[section, inner, j]).wait_send()
+
+            for copy in partner_copies(section, 0, inner, j, held.at[section, inner, j]):
+                copy.wait_send()
+            inner_far = mirror_inner(n)
+
+            @pl.when(within(mirror, inner_far, j, left))
+            def _():
+                for copy in partner_copies(mirror, 1, inner_far, j, held.at[mirror, inner_far, j]):
                     copy.wait_send()
 
 
@@ -413,6 +456,7 @@
             pltpu.VMEM((2, own_x, size // 2, size), F32),
             dma((sections, own_x, tiles)),
             dma((own_x, tiles)),
+            dma((own_x, tiles)),
             dma((2, tiles)),
             dma((own_x, tiles)),
             dma((2, max(sections // 2 - 1, 1), own_x, tiles)),

time: 43.1 us -> 44.9 us (1.042)
  Pallas kernels: 41.2 us -> 43.1 us
    pallas_call x1, Pallas kernels: 41.2 us -> 43.1 us  [on_device(): pl.pallas_call(functools.partial(kernel, tiles, sections), out_shape=jax....]
where the time goes in v4:
time: 44.9 us; the launch traced here: 44.7 us
  Pallas kernels  43.1 us (96%)
  local copies, waits for them, and re-layouts  1.57 us (3%)
    pallas_call x1, Pallas kernels, on_device(): pl.pallas_call(functools.partial(kernel, tiles, sections), out_shape=jax....  43.1 us
    unnamed x1, local copies, waits for them, and re-layouts  1.57 us

profile of v4, /device:TPU:0, one launch (start us, length us, event | category | flops | bytes accessed | tf_op | source)
XLA Modules:
  0.0 44.7 jit_solution(2856116591667730612)
XLA Ops:
  0.0 43.1 %shard_map.73 = f32[2,128,128]{2,1,0:T(8,128)} custom-call(s32[2,128,128]{2,1,0:T(8,128)} %labels_ref.1, s32[2,128,128]{2,1,0:T(8,128)} %classes_ref.1, s32[4]{0:T(128)} %pos_ref.1, f32[8]{0:T(128)} %phase_ref.1, f32[16]{0:T(128)} %bright_ref.1, f32[2,2,129]{2,1,0:T(2,128)} %prop_ref.1, f32[2,129]{1,0:T(2,128)} %detect_ref.1), custom_call_target="tpu_custom_call" | custom-call | tf_op jit(solution)/shard_map/pallas_call | solution.py:438
  43.1 1.6 %copy.9 = f32[2,128,128]{2,1,0:T(8,128)} copy(f32[2,128,128]{2,1,0:T(8,128)} %shard_map.73) | data formatting | bytes 262144
